TPU v7x, 128 devices: a whole 4x4x4 slice. The times are simulated.
128 devices in a mesh: row: 8 (over y, core), col: 16 (over z, x).
Axes of the slice: x: 4, y: 4, z: 4, core: 2. Of those that a mesh axis runs over, the one named last changes fastest.
Arguments:
- hidden_states: bfloat16 [1024, 2048], P('col', 'row'), may hold values from -20 to 20
- input_gain: float32 [2, 2048], P(None, 'row'), may hold values from 0.25 to 1.75
- inner_weight: bfloat16 [2, 2048, 2, 4096], P(None, 'row', None, 'col'), may hold values from -0.125 to 0.125
- proj_weight: bfloat16 [2, 2048, 256], P(None, 'row'), may hold values from -0.125 to 0.125
- step_weight: bfloat16 [2, 2048, 64], P(None, 'row', 'col'), may hold values from -0.125 to 0.125
- inner_kernel: float32 [2, 4, 4096], P(None, None, 'col'), may hold values from -3 to 3
- proj_kernel: float32 [2, 4, 256], replicated, may hold values from -3 to 3
- step_bias: float32 [2, 64], P(None, 'col'), may hold values from -5 to -1
- decay_log: float32 [2, 64], P(None, 'col'), may hold values from -2 to 1
- skip_gain: float32 [2, 64], P(None, 'col'), may hold values from 0.5 to 1.5
- norm_gain: float32 [2, 4096], P(None, 'col'), may hold values from 0.25 to 1.75
- out_weight: bfloat16 [2, 4096, 2048], P(None, 'col', 'row'), may hold values from -0.09375 to 0.09375
- inner_cache: bfloat16 [2, 64, 3, 4096], P(None, 'row', None, 'col'), may hold values from -6 to 6
- proj_cache: bfloat16 [2, 64, 3, 256], P(None, 'row'), may hold values from -6 to 6
- state_cache: float32 [2, 64, 64, 64, 128], P(None, 'row', 'col'), may hold values from -1.2 to 1.2
- accepted: int32 [64], P('row'), may hold values from 1 to 16
- owners: int32 [64], P('row'), may hold values from 0 to 15, as said below
- tenant_ranges: int32 [4, 2], replicated, may hold values from 0 to 64, as said below
Outputs:
- hidden_output: bfloat16 [1024, 2048], P('col', 'row')
- step_states: bfloat16 [2, 64, 16, 64, 64, 128], P(None, 'row', None, 'col')
- owned_states: bfloat16 [8, 16, 2, 2, 64, 64, 128], P('row', 'col')
Inputs may be any that keep to these rules, and one draw needn't show every extreme that they name: `owners`: within the requests of one index of row (aligned blocks of 8) no owner appears more than 2 times, and in every block some owner appears exactly 2 times. `tenant_ranges`: the ranges are in order, disjoint and not empty; exactly 8 requests lie in no range.
All inputs are finite; a program needn't handle non-finite values.
Results may differ from a plain program's by a relative error of at most 0.024.
Values may be sent and summed in bfloat16 or wider, within the bound.
No kernel may reach another device: no remote copies, remote signals or barrier semaphores. Data moves between devices by JAX's collectives and lax.ppermute only.
A program may use at most 128 MiB of HBM per device.

v0:
```python
import jax
import jax.numpy as jnp
from jax import lax
from jax.sharding import PartitionSpec as P

S = 16
SEND_CAP = 2
EPSILON = 1e-05


def conv_silu(prefix, incoming, kernel):
    joined = jnp.concatenate([prefix, incoming], axis=1)
    length = incoming.shape[1]
    summed = joined[:, 0:length, :] * kernel[0]
    for offset in range(1, kernel.shape[0]):
        summed = summed + joined[:, offset : offset + length, :] * kernel[offset]
    return jax.nn.silu(summed)


def ssm_scan(decays, deltas, inner_values, b_values, c_values, skip_values, start_state):

    def advance(carried, packed):
        decay_now, delta_now, value_now, b_now, c_now = packed
        updated = (
            decay_now[:, :, None, None] * carried
            + (delta_now[:, :, None] * value_now)[:, :, :, None] * b_now[:, None, None, :]
        )
        output = (
            jnp.einsum("rhpn,rn->rhp", updated, c_now, precision=lax.Precision.HIGHEST)
            + skip_values[None, :, None] * value_now
        )
        return (updated, (output, updated.astype(jnp.bfloat16)))

    time_major = tuple(
        (
            jnp.moveaxis(member, 1, 0)
            for member in (decays, deltas, inner_values, b_values, c_values)
        )
    )
    last_state, (outputs, states) = lax.scan(advance, start_state, time_major)
    return (jnp.moveaxis(outputs, 0, 1), jnp.moveaxis(states, 0, 1))


def local(
    hidden_states,
    input_gain,
    inner_weight,
    proj_weight,
    step_weight,
    inner_kernel,
    proj_kernel,
    step_bias,
    decay_log,
    skip_gain,
    norm_gain,
    out_weight,
    inner_cache,
    proj_cache,
    state_cache,
    accepted,
    owners,
    tenant_ranges,
):
    layer_count = inner_weight.shape[0]
    row_width = inner_weight.shape[1]
    inner_local = inner_weight.shape[3]
    heads_local = step_weight.shape[2]
    head_size = inner_local // heads_local
    state_size = proj_weight.shape[2] // 2
    requests_local = state_cache.shape[1]
    draft_steps = S
    row_count = lax.axis_size("row")
    col_count = lax.axis_size("col")
    model_width = row_width * row_count
    inner_width = inner_local * col_count
    token_rows = requests_local * draft_steps
    local_ids = jnp.arange(requests_local, dtype=jnp.int32)
    request_ids = lax.axis_index("row") * requests_local + local_ids
    live_mask = jnp.any(
        (request_ids[:, None] >= tenant_ranges[None, :, 0])
        & (request_ids[:, None] < tenant_ranges[None, :, 1]),
        axis=1,
    )
    earlier = (owners[:, None] == owners[None, :]) & (local_ids[None, :] < local_ids[:, None])
    slot_ranks = jnp.sum(earlier.astype(jnp.int32), axis=1)
    slot_ids = owners * SEND_CAP + slot_ranks
    slot_grid = jnp.arange(col_count * SEND_CAP, dtype=jnp.int32)
    step_grid = jnp.arange(draft_steps, dtype=jnp.int32)
    picker = (
        (slot_grid[:, None, None] == slot_ids[None, :, None])
        & (step_grid[None, None, :] == accepted[None, :, None] - 1)
        & live_mask[None, :, None]
    )
    picker = picker.astype(jnp.bfloat16).reshape(col_count * SEND_CAP, token_rows)
    hidden = hidden_states
    step_outputs = []
    chosen_layers = []
    for layer_index in range(layer_count):
        all_tokens = lax.all_gather(hidden, "col", axis=0, tiled=True)
        tokens_f = all_tokens.astype(jnp.float32)
        scaled = (tokens_f * input_gain[layer_index]).astype(jnp.bfloat16)
        square_part = jnp.sum(tokens_f * tokens_f, axis=1)
        inner_part = jnp.dot(
            scaled,
            inner_weight[layer_index].reshape(row_width, 2 * inner_local),
            preferred_element_type=jnp.float32,
        )
        step_part = jnp.dot(scaled, step_weight[layer_index], preferred_element_type=jnp.float32)
        proj_part = jnp.dot(scaled, proj_weight[layer_index], preferred_element_type=jnp.float32)
        inner_sum, step_sum, proj_sum, square_sum = (
            lax.psum_scatter(inner_part, "row", scatter_dimension=0, tiled=True),
            lax.psum_scatter(step_part, "row", scatter_dimension=0, tiled=True),
            lax.psum_scatter(proj_part, "row", scatter_dimension=0, tiled=True),
            lax.psum_scatter(square_part, "row", scatter_dimension=0, tiled=True),
        )
        inverse_rms = lax.rsqrt(square_sum / model_width + EPSILON)
        inner_vals = inner_sum * inverse_rms[:, None]
        gate_vals = inner_vals[:, :inner_local]
        raw_inner = inner_vals[:, inner_local:].reshape(requests_local, draft_steps, inner_local)
        raw_proj = (proj_sum * inverse_rms[:, None]).reshape(
            requests_local, draft_steps, 2 * state_size
        )
        conv_inner = conv_silu(
            inner_cache[layer_index].astype(jnp.float32), raw_inner, inner_kernel[layer_index]
        )
        conv_proj = conv_silu(
            proj_cache[layer_index].astype(jnp.float32), raw_proj, proj_kernel[layer_index]
        )
        deltas = jax.nn.softplus(
            (step_sum * inverse_rms[:, None]).reshape(requests_local, draft_steps, heads_local)
            + step_bias[layer_index]
        )
        decays = jnp.exp(-deltas * jnp.exp(decay_log[layer_index]))
        outputs, states = ssm_scan(
            decays,
            deltas,
            conv_inner.reshape(requests_local, draft_steps, heads_local, head_size),
            conv_proj[..., :state_size],
            conv_proj[..., state_size:],
            skip_gain[layer_index],
            state_cache[layer_index],
        )
        step_outputs.append(states)
        gated_raw = outputs.reshape(token_rows, inner_local) * jax.nn.silu(gate_vals)
        gate_square = lax.psum(jnp.sum(gated_raw * gated_raw, axis=1), "col")
        gated = (
            gated_raw
            * norm_gain[layer_index]
            * lax.rsqrt(gate_square / inner_width + EPSILON)[:, None]
        ).astype(jnp.bfloat16)
        layer_weight = out_weight[layer_index]
        partial_out = jnp.dot(
            lax.all_gather(gated, "row", axis=0, tiled=True),
            layer_weight,
            preferred_element_type=jnp.float32,
        )
        out_sum = lax.psum_scatter(
            partial_out.astype(jnp.bfloat16), "col", scatter_dimension=0, tiled=True
        ).astype(jnp.float32)
        hidden = (hidden.astype(jnp.float32) + out_sum).astype(jnp.bfloat16)
        chosen = jnp.dot(
            picker,
            states.reshape(token_rows, heads_local * head_size * state_size),
            preferred_element_type=jnp.float32,
        )
        chosen = chosen.astype(jnp.bfloat16).reshape(
            col_count, SEND_CAP, heads_local, head_size, state_size
        )
        chosen_layers.append(chosen)
    gathered = lax.all_to_all(
        jnp.stack(chosen_layers, axis=2), "col", split_axis=0, concat_axis=3, tiled=True
    )
    owned_block = gathered[None]
    step_all = jnp.stack(step_outputs, axis=0)
    return (hidden, step_all, owned_block)


def solution(mesh):
    placed = (
        P("col", "row"),
        P(None, "row"),
        P(None, "row", None, "col"),
        P(None, "row", None),
        P(None, "row", "col"),
        P(None, None, "col"),
        P(),
        P(None, "col"),
        P(None, "col"),
        P(None, "col"),
        P(None, "col"),
        P(None, "col", "row"),
        P(None, "row", None, "col"),
        P(None, "row", None, None),
        P(None, "row", "col", None, None),
        P("row"),
        P("row"),
        P(),
    )
    return jax.shard_map(
        local,
        mesh=mesh,
        in_specs=placed,
        out_specs=(
            P("col", "row"),
            P(None, "row", None, "col", None, None),
            P("row", "col", None, None, None, None, None),
        ),
        check_vma=False,
    )
```

profile of v0, /device:TPU:0, one launch (start us, length us, event | category | flops | bytes accessed | tf_op | source)
XLA Modules:
  0.0 788.9 jit_solution(10721165272953729870)
XLA Ops:
  8.6 25.4 %all_gather.12 = bf16[1024,256]{1,0:T(8,128)(2,1)S(1)} all-gather(bf16[64,256]{1,0:T(8,128)(2,1)} %param.22), channel_id=1, replica_groups=mesh['row'=8,'col'=16] {'col'}, dimensions={0}, use_global_device_ids=true | all-gather | bytes 557056 | tf_op jit(solution)/shard_map/all_gather | solution.py:99
  42.9 12.5 %all-reduce = f32[1024]{0:T(1024)S(1)} all-reduce(f32[1024]{0:T(1024)S(1)} %fusion.5), channel_id=3, replica_groups=mesh['row'=8,'col'=16] {'row'}, use_global_device_ids=true, to_apply=%region_2.0.clone | all-reduce | flops 1024 | bytes 8192
  60.8 5.6 reduce-scatter.25.cloned.1.call-done
  69.0 31.3 %reduce-scatter.15.cloned.1.call-done = f32[128,256]{1,0:T(8,128)} async-done(((f32[1024,256]{1,0:T(8,128)}), f32[128,256]{1,0:T(8,128)}) %reduce-scatter.15.cloned.1.call-update) | async-done | bytes 131088 | tf_op jit(solution)/shard_map/reduce_scatter | solution.py:113
  102.1 33.8 %reduce-scatter.13.cloned.1.call-done = f32[128,512]{1,0:T(8,128)} async-done(((f32[1024,512]{1,0:T(8,128)}), f32[128,512]{1,0:T(8,128)}) %reduce-scatter.13.cloned.1.call-update) | async-done | bytes 262160 | tf_op jit(solution)/shard_map/reduce_scatter | solution.py:111
  137.4 5.4 broadcast.153.clone2
  142.7 103.3 %while.28 = (s32[]{:T(128)}, f32[8,4,64,128]{3,2,1,0:T(8,128)S(1)}, f32[16,8,4,64]{3,2,1,0:T(4,128)S(1)}, bf16[16,8,4,64,128]{4,3,2,0,1:T(8,128)(2,1)}, f32[16,8...) while((s32[]{:T(128)}, f32[8,4,64,128]{3,2,1,0:T(8,128)S(1)}, ...), condition=%wide.region_6.0_spmd, body=%wide.region_5.0_spmd.sunk | while | flops 4200450 | bytes 3777949 | solution.py:40
  145.9 2.5 fusion.99
  158.8 2.5 fusion.99
  165.3 2.5 fusion.99
  171.7 2.5 fusion.99
  178.2 2.5 fusion.99
  184.6 2.5 fusion.99
  246.5 40.5 %psum.14 = f32[128]{0:T(128)S(1)} all-reduce(f32[128]{0:T(128)S(1)} %get-tuple-element.179), channel_id=1, replica_groups=mesh['row'=8,'col'=16] {'col'}, use_global_device_ids=true, to_apply=%region_8.9 | all-reduce | flops 128 | bytes 1024 | tf_op jit(solution)/shard_map/psum | solution.py:145
  287.8 13.1 %all_gather.13 = bf16[1024,256]{1,0:T(8,128)(2,1)S(1)} all-gather(bf16[128,256]{1,0:T(8,128)(2,1)S(1)} %multiply_convert_fusion.1), channel_id=1, replica_groups=mesh['row'=8,'col'=16] {'row'}, dimensions={0}, use_global_device_ids=true | all-gather | bytes 589824 | tf_op jit(solution)/shard_map/all_gather | solution.py:153
  302.9 67.3 %reduce-scatter.17.cloned.1.call-done = bf16[64,256]{1,0:T(8,128)(2,1)} async-done(((bf16[1024,256]{1,0:T(8,128)(2,1)}), bf16[64,256]{1,0:T(8,128)(2,1)}) %reduce-scatter.17.cloned.1.call-update) | async-done | bytes 32784 | tf_op jit(solution)/shard_map/reduce_scatter | solution.py:157
  371.0 23.3 %all_gather.14 = bf16[1024,256]{1,0:T(8,128)(2,1)S(1)} all-gather(bf16[64,256]{1,0:T(8,128)(2,1)S(1)} %add_convert_fusion.1), channel_id=1, replica_groups=mesh['row'=8,'col'=16] {'col'}, dimensions={0}, use_global_device_ids=true | all-gather | bytes 557056 | tf_op jit(solution)/shard_map/all_gather | solution.py:99
  400.6 13.3 %reshape.291 = bf16[128,32768]{1,0:T(8,128)(2,1)} reshape(bf16[8,16,4,64,128]{4,3,2,1,0:T(8,128)(2,1)} %bitcast.249) | data formatting | bytes 16777216 | tf_op jit(solution)/shard_map/reshape | solution.py:163
  414.0 4.7 fusion.2
  420.7 12.6 %all-reduce.1 = f32[1024]{0:T(1024)S(1)} all-reduce(f32[1024]{0:T(1024)S(1)} %fusion.7), channel_id=8, replica_groups=mesh['row'=8,'col'=16] {'row'}, use_global_device_ids=true, to_apply=%region_12.13.clone | all-reduce | flops 1024 | bytes 8192
  434.7 24.2 %reduce-scatter.21.cloned.1.call-done = f32[128,256]{1,0:T(8,128)} async-done(((f32[1024,256]{1,0:T(8,128)}), f32[128,256]{1,0:T(8,128)}) %reduce-scatter.21.cloned.1.call-update) | async-done | bytes 131088 | tf_op jit(solution)/shard_map/reduce_scatter | solution.py:113
  460.1 34.4 %reduce-scatter.19.cloned.1.call-done = f32[128,512]{1,0:T(8,128)} async-done(((f32[1024,512]{1,0:T(8,128)}), f32[128,512]{1,0:T(8,128)}) %reduce-scatter.19.cloned.1.call-update) | async-done | bytes 262160 | tf_op jit(solution)/shard_map/reduce_scatter | solution.py:111
  496.0 5.4 broadcast.153.clone
  501.4 70.9 %while.29 = (s32[]{:T(128)}, f32[8,4,64,128]{3,2,1,0:T(8,128)S(1)}, f32[16,8,4,64]{3,2,1,0:T(4,128)S(1)}, bf16[16,8,4,64,128]{4,3,2,0,1:T(8,128)(2,1)}, f32[16,8...) while((s32[]{:T(128)}, f32[8,4,64,128]{3,2,1,0:T(8,128)S(1)}, ...), condition=%wide.region_16.17_spmd, body=%wide.region_15.16_spmd.sunk | while | flops 4200450 | bytes 3778445 | solution.py:40
  572.4 13.3 %reshape.292 = bf16[128,32768]{1,0:T(8,128)(2,1)} reshape(bf16[8,16,4,64,128]{4,3,2,1,0:T(8,128)(2,1)} %bitcast.247) | data formatting | bytes 16777216 | tf_op jit(solution)/shard_map/reshape | solution.py:163
  585.6 4.8 fusion.3
  593.3 7.0 all-to-all-start
  600.8 81.9 %psum.15 = f32[128]{0:T(128)S(1)} all-reduce(f32[128]{0:T(128)S(1)} %get-tuple-element.177), channel_id=1, replica_groups=mesh['row'=8,'col'=16] {'col'}, use_global_device_ids=true, to_apply=%region_18.19 | all-reduce | flops 128 | bytes 1024 | tf_op jit(solution)/shard_map/psum | solution.py:145
  682.8 21.8 %all_gather.15 = bf16[1024,256]{1,0:T(8,128)(2,1)S(1)} all-gather(bf16[128,256]{1,0:T(8,128)(2,1)S(1)} %multiply_convert_fusion), channel_id=1, replica_groups=mesh['row'=8,'col'=16] {'row'}, dimensions={0}, use_global_device_ids=true | all-gather | bytes 589824 | tf_op jit(solution)/shard_map/all_gather | solution.py:153
  705.7 13.8 %pad_maximum_fusion = bf16[2,8,16,4,64,128]{5,4,3,2,1,0:T(8,128)(2,1)} fusion(bf16[1,8,16,4,64,128]{5,4,3,2,1,0:T(8,128)(2,1)} %bitcast.248, bf16[1,8,16,4,64,128]{5,4,3,2,1,0:T(8,128)(2,1)} %bitcast.250), kind=kLoop, calls=%fused_computation.22 | loop fusion | flops 8388608 | bytes 33554432 | tf_op jit(solution)/shard_map/stack | solution.py:174
  719.5 55.1 %reduce-scatter.23.cloned.1.call-done = bf16[64,256]{1,0:T(8,128)(2,1)} async-done(((bf16[1024,256]{1,0:T(8,128)(2,1)}), bf16[64,256]{1,0:T(8,128)(2,1)}) %reduce-scatter.23.cloned.1.call-update) | async-done | bytes 32784 | tf_op jit(solution)/shard_map/reduce_scatter | solution.py:157
  776.1 6.0 copy.143
  (439 shorter events, 201.0 us)
Async XLA Ops:
  7.2 48.3 %copy-start.22 = (f32[2,4]{1,0:T(2,128)S(1)}, f32[2,4]{1,0:T(2,128)}, u32[]{:S(2)}) copy-start(f32[2,4]{1,0:T(2,128)} %param.31) | copy-start | bytes 100
  7.2 48.9 %copy-start.21 = (f32[2,256]{1,0:T(2,128)S(1)}, f32[2,256]{1,0:T(2,128)}, u32[]{:S(2)}) copy-start(f32[2,256]{1,0:T(2,128)} %param.32) | copy-start | bytes 6148
  7.2 49.5 %copy-start.25 = (f32[2,4]{1,0:T(2,128)S(1)}, f32[2,4]{1,0:T(2,128)}, u32[]{:S(2)}) copy-start(f32[2,4]{1,0:T(2,128)} %param.30) | copy-start | bytes 100
  7.2 49.5 %copy-start.24 = (f32[2,4]{1,0:T(2,128)S(1)}, f32[2,4]{1,0:T(2,128)}, u32[]{:S(2)}) copy-start(f32[2,4]{1,0:T(2,128)} %param.29) | copy-start | bytes 100
  7.2 50.0 %copy-start.8 = (f32[2,4,256]{2,1,0:T(4,128)S(1)}, f32[2,4,256]{2,1,0:T(4,128)}, u32[]{:S(2)}) copy-start(f32[2,4,256]{2,1,0:T(4,128)} %param.27) | copy-start | bytes 24580
  7.2 50.6 %copy-start.9 = (f32[2,4,256]{2,1,0:T(4,128)S(1)}, f32[2,4,256]{2,1,0:T(4,128)}, u32[]{:S(2)}) copy-start(f32[2,4,256]{2,1,0:T(4,128)} %param.28) | copy-start | bytes 24580
  7.2 51.2 %copy-start.5 = (bf16[2,8,3,256]{3,1,2,0:T(8,128)(2,1)S(1)}, bf16[2,8,3,256]{3,1,2,0:T(8,128)(2,1)}, u32[]{:S(2)}) copy-start(bf16[2,8,3,256]{3,1,2,0:T(8,128)(2,1)} %param.34) | copy-start | bytes 73732
  7.3 51.2 %copy-start.6 = (bf16[2,8,3,256]{3,1,2,0:T(8,128)(2,1)S(1)}, bf16[2,8,3,256]{3,1,2,0:T(8,128)(2,1)}, u32[]{:S(2)}) copy-start(bf16[2,8,3,256]{3,1,2,0:T(8,128)(2,1)} %param.35) | copy-start | bytes 73732
  7.3 59.2 %reduce-scatter.25.cloned.1.call-start = ((), (), s32[]{:S(2)}) async-start(), calls=%async_computation.15 | async-start | bytes 589824
  35.9 64.4 %reduce-scatter.15.cloned.1.call-start = ((), (), s32[]{:S(2)}) async-start(), calls=%async_computation.10 | async-start | bytes 1179648 | tf_op jit(solution)/shard_map/reduce_scatter | solution.py:113
  38.1 97.8 %reduce-scatter.13.cloned.1.call-start = ((), (), s32[]{:S(2)}) async-start(), calls=%async_computation.9 | async-start | bytes 2359296 | tf_op jit(solution)/shard_map/reduce_scatter | solution.py:111
  41.4 328.8 %reduce-scatter.17.cloned.1.call-start = ((), (), s32[]{:S(2)}) async-start(), calls=%async_computation.11 | async-start | bytes 557056 | tf_op jit(solution)/shard_map/reduce_scatter | solution.py:157
  142.7 227.5 %copy-start.3 = (bf16[64,256]{1,0:T(8,128)(2,1)S(1)}, bf16[64,256]{1,0:T(8,128)(2,1)}, u32[]{:S(2)}) copy-start(bf16[64,256]{1,0:T(8,128)(2,1)} %param.22) | copy-start | bytes 98308
  142.7 253.4 %copy-start.1 = (bf16[2,256,256]{2,1,0:T(8,128)(2,1)S(1)}, bf16[2,256,256]{2,1,0:T(8,128)(2,1)}, u32[]{:S(2)}) copy-start(bf16[2,256,256]{2,1,0:T(8,128)(2,1)} %param.25) | copy-start | bytes 786436
  246.1 152.2 %copy-start.7 = (f32[1,256]{1,0:T(1,128)S(1)}, f32[1,256]{1,0:T(1,128)}, u32[]{:S(2)}) copy-start(f32[1,256]{1,0:T(1,128)} %get-tuple-element.219) | copy-start | bytes 3076
  246.1 154.0 %copy-start.27 = (s32[8]{0:T(128)S(1)}, s32[8]{0:T(128)}, u32[]{:S(2)}) copy-start(s32[8]{0:T(128)} %param.38) | copy-start | bytes 100
  246.1 154.2 %copy-start.23 = (s32[4,2]{0,1:T(2,128)S(1)}, s32[4,2]{0,1:T(2,128)}, u32[]{:S(2)}) copy-start(s32[4,2]{0,1:T(2,128)} %param.39) | copy-start | bytes 100
  246.1 154.3 %copy-start.26 = (s32[8]{0:T(128)S(1)}, s32[8]{0:T(128)}, u32[]{:S(2)}) copy-start(s32[8]{0:T(128)} %param.37) | copy-start | bytes 100
  302.9 130.5 %reduce-scatter.27.cloned.1.call-start = ((), (), s32[]{:S(2)}) async-start(), calls=%async_computation.16 | async-start | bytes 589824
  396.1 62.8 %reduce-scatter.21.cloned.1.call-start = ((), (), s32[]{:S(2)}) async-start(), calls=%async_computation.13 | async-start | bytes 1179648 | tf_op jit(solution)/shard_map/reduce_scatter | solution.py:113
  398.2 96.4 %reduce-scatter.19.cloned.1.call-start = ((), (), s32[]{:S(2)}) async-start(), calls=%async_computation.12 | async-start | bytes 2359296 | tf_op jit(solution)/shard_map/reduce_scatter | solution.py:111
  413.9 46.1 %copy-start.15 = (f32[1,1,256]{2,1,0:T(1,128)S(1)}, f32[1,1,256]{2,1,0:T(1,128)}, u32[]{:S(2)}) copy-start(f32[1,1,256]{2,1,0:T(1,128)} %get-tuple-element.202) | copy-start | bytes 3076
  413.9 46.1 %copy-start.16 = (f32[1,1,256]{2,1,0:T(1,128)S(1)}, f32[1,1,256]{2,1,0:T(1,128)}, u32[]{:S(2)}) copy-start(f32[1,1,256]{2,1,0:T(1,128)} %get-tuple-element.207) | copy-start | bytes 3076
  413.9 46.1 %copy-start.17 = (f32[1,1,256]{2,1,0:T(1,128)S(1)}, f32[1,1,256]{2,1,0:T(1,128)}, u32[]{:S(2)}) copy-start(f32[1,1,256]{2,1,0:T(1,128)} %get-tuple-element.208) | copy-start | bytes 3076
  414.0 81.8 %copy-start.10 = (f32[1,1,256]{2,1,0:T(1,128)S(1)}, f32[1,1,256]{2,1,0:T(1,128)}, u32[]{:S(2)}) copy-start(f32[1,1,256]{2,1,0:T(1,128)} %get-tuple-element.209) | copy-start | bytes 3076
  414.0 81.8 %copy-start.11 = (f32[1,1,256]{2,1,0:T(1,128)S(1)}, f32[1,1,256]{2,1,0:T(1,128)}, u32[]{:S(2)}) copy-start(f32[1,1,256]{2,1,0:T(1,128)} %get-tuple-element.210) | copy-start | bytes 3076
  414.0 81.8 %copy-start.12 = (f32[1,1,256]{2,1,0:T(1,128)S(1)}, f32[1,1,256]{2,1,0:T(1,128)}, u32[]{:S(2)}) copy-start(f32[1,1,256]{2,1,0:T(1,128)} %get-tuple-element.215) | copy-start | bytes 3076
  414.0 81.8 %copy-start.13 = (f32[1,1,256]{2,1,0:T(1,128)S(1)}, f32[1,1,256]{2,1,0:T(1,128)}, u32[]{:S(2)}) copy-start(f32[1,1,256]{2,1,0:T(1,128)} %get-tuple-element.216) | copy-start | bytes 3076
  590.9 91.8 %copy-start.18 = (f32[1,256]{1,0:T(1,128)S(1)}, f32[1,256]{1,0:T(1,128)}, u32[]{:S(2)}) copy-start(f32[1,256]{1,0:T(1,128)} %get-tuple-element.217) | copy-start | bytes 3076
  590.9 113.7 %copy-start.2 = (bf16[2,256,256]{2,1,0:T(8,128)(2,1)S(1)}, bf16[2,256,256]{2,1,0:T(8,128)(2,1)}, u32[]{:S(2)}) copy-start(bf16[2,256,256]{2,1,0:T(8,128)(2,1)} %param.33) | copy-start | bytes 786436
  593.3 182.7 %all-to-all-start = ((bf16[16,2,2,4,64,128]{5,4,3,1,2,0:T(8,128)(2,1)}), bf16[16,2,2,4,64,128]{5,4,3,1,2,0:T(8,128)(2,1)}, u32[]{:S(2)}, u32[]{:S(2)}) async-start(bf16[16,2,2,4,64,128]{5,4,3,1,2,0:T(8,128)(2,1)} %pad_maximum_fusion.1), calls=%async_computation.6 | async-start | bytes 8388608 | tf_op jit(solution)/shard_map/all_to_all | solution.py:170
  600.3 174.4 %reduce-scatter.23.cloned.1.call-start = ((), (), s32[]{:S(2)}) async-start(), calls=%async_computation.14 | async-start | bytes 557056 | tf_op jit(solution)/shard_map/reduce_scatter | solution.py:157
  (6 other events, 172.7 us)
Sparse Core Ops, SparseCore 0:
  36.0 30.4 reduce-scatter.24
  69.5 30.7 reduce-scatter.14
  103.4 32.4 reduce-scatter.12
  303.0 67.1 reduce-scatter.16
  396.2 29.5 reduce-scatter.26
  428.2 30.6 reduce-scatter.20
  462.0 32.5 reduce-scatter.18
  705.8 68.7 reduce-scatter.22
where the time goes:
time: 792 us; the launch traced here: 789 us
  waiting for transfers between devices  252 us (32%)
  blocking collectives  231 us (29%)
  matrix products  105 us (13%)
  other arithmetic  90.8 us (11%)
  local copies, waits for them, and re-layouts  86.9 us (11%)
  between operations  15.4 us (2%)
    psum x2, blocking collectives, local(): gate_square = lax.psum(jnp.sum(gated_raw * gated_raw, axis=1), 'col')  122 us
    reduce_scatter x2, waiting for transfers between devices, local(): lax.psum_scatter(partial_out.astype(jnp.bfloat16), 'col', scatter_dimensi...  122 us
    dot_general x32, matrix products, advance(): jnp.einsum('rhpn,rn->rhp', updated, c_now, precision=lax.Precision.HIGHEST)  80.9 us
    reduce_scatter x2, waiting for transfers between devices, local(): lax.psum_scatter(inner_part, 'row', scatter_dimension=0, tiled=True)  68.3 us
    dynamic_update_slice x64, other arithmetic, ssm_scan(): last_state, (outputs, states) = lax.scan(advance, start_state, time_major)  62.7 us
    reduce_scatter x2, waiting for transfers between devices, local(): lax.psum_scatter(proj_part, 'row', scatter_dimension=0, tiled=True)  55.6 us
    all_gather x2, blocking collectives, local(): all_tokens = lax.all_gather(hidden, 'col', axis=0, tiled=True)  48.8 us
    all_gather x2, blocking collectives, local(): lax.all_gather(gated, 'row', axis=0, tiled=True)  34.9 us
  transfers between devices with their start and end apart: 9, of which 7 were waited for; matrix products, arithmetic and copies ran while one was open for 8% of the time, Pallas kernels for 0%

commit v1 on v0

--- a/solution.py
+++ b/solution.py
@@ -142,7 +142,7 @@
         )
         step_outputs.append(states)
         gated_raw = outputs.reshape(token_rows, inner_local) * jax.nn.silu(gate_vals)
-        gate_square = lax.psum(jnp.sum(gated_raw * gated_raw, axis=1), "col")
+        gate_square = jnp.sum(lax.all_gather(jnp.sum(gated_raw * gated_raw, axis=1), "col"), axis=0)
         gated = (
             gated_raw
             * norm_gain[layer_index]

time: 792 us -> 761 us (0.961)
  blocking collectives: 231 us -> 194 us
    psum x2 -> x0, blocking collectives: 122 us -> none  [local(): gate_square = lax.psum(jnp.sum(gated_raw * gated_raw, axis=1), 'col')]
    all_gather x0 -> x2, blocking collectives: none -> 86.9 us  [local(): lax.all_gather(jnp.sum(gated_raw * gated_raw, axis=1), 'col')]
where the time goes in v1:
time: 761 us; the launch traced here: 758 us
  waiting for transfers between devices  259 us (34%)
  blocking collectives  194 us (25%)
  matrix products  105 us (14%)
  other arithmetic  90.9 us (12%)
  local copies, waits for them, and re-layouts  86.9 us (11%)
  between operations  15.4 us (2%)
    reduce_scatter x2, waiting for transfers between devices, local(): lax.psum_scatter(partial_out.astype(jnp.bfloat16), 'col', scatter_dimensi...  129 us
    all_gather x2, blocking collectives, local(): lax.all_gather(jnp.sum(gated_raw * gated_raw, axis=1), 'col')  86.9 us
    dot_general x32, matrix products, advance(): jnp.einsum('rhpn,rn->rhp', updated, c_now, precision=lax.Precision.HIGHEST)  80.9 us
    reduce_scatter x2, waiting for transfers between devices, local(): lax.psum_scatter(inner_part, 'row', scatter_dimension=0, tiled=True)  68.3 us
    dynamic_update_slice x64, other arithmetic, ssm_scan(): last_state, (outputs, states) = lax.scan(advance, start_state, time_major)  62.7 us
    reduce_scatter x2, waiting for transfers between devices, local(): lax.psum_scatter(proj_part, 'row', scatter_dimension=0, tiled=True)  55.5 us
    all_gather x2, blocking collectives, local(): all_tokens = lax.all_gather(hidden, 'col', axis=0, tiled=True)  48.8 us
    all_gather x2, blocking collectives, local(): lax.all_gather(gated, 'row', axis=0, tiled=True)  33 us
  transfers between devices with their start and end apart: 9, of which 7 were waited for; matrix products, arithmetic and copies ran while one was open for 8% of the time, Pallas kernels for 0%

profile of v1, /device:TPU:0, one launch (start us, length us, event | category | flops | bytes accessed | tf_op | source)
XLA Modules:
  0.0 758.3 jit_solution(8419386296595267680)
XLA Ops:
  8.6 25.4 %all_gather.24 = bf16[1024,256]{1,0:T(8,128)(2,1)S(1)} all-gather(bf16[64,256]{1,0:T(8,128)(2,1)} %param.22), channel_id=1, replica_groups=mesh['row'=8,'col'=16] {'col'}, dimensions={0}, use_global_device_ids=true | all-gather | bytes 557056 | tf_op jit(solution)/shard_map/all_gather | solution.py:99
  42.9 12.5 %all-reduce = f32[1024]{0:T(1024)S(1)} all-reduce(f32[1024]{0:T(1024)S(1)} %fusion.5), channel_id=5, replica_groups=mesh['row'=8,'col'=16] {'row'}, use_global_device_ids=true, to_apply=%region_2.0.clone | all-reduce | flops 1024 | bytes 8192
  60.8 5.6 reduce-scatter.25.cloned.1.call-done
  69.0 31.3 %reduce-scatter.15.cloned.1.call-done = f32[128,256]{1,0:T(8,128)} async-done(((f32[1024,256]{1,0:T(8,128)}), f32[128,256]{1,0:T(8,128)}) %reduce-scatter.15.cloned.1.call-update) | async-done | bytes 131088 | tf_op jit(solution)/shard_map/reduce_scatter | solution.py:113
  102.1 33.8 %reduce-scatter.13.cloned.1.call-done = f32[128,512]{1,0:T(8,128)} async-done(((f32[1024,512]{1,0:T(8,128)}), f32[128,512]{1,0:T(8,128)}) %reduce-scatter.13.cloned.1.call-update) | async-done | bytes 262160 | tf_op jit(solution)/shard_map/reduce_scatter | solution.py:111
  137.4 5.4 broadcast.167.clone2
  142.7 103.3 %while.28 = (s32[]{:T(128)}, f32[8,4,64,128]{3,2,1,0:T(8,128)S(1)}, f32[16,8,4,64]{3,2,1,0:T(4,128)S(1)}, bf16[16,8,4,64,128]{4,3,2,0,1:T(8,128)(2,1)}, f32[16,8...) while((s32[]{:T(128)}, f32[8,4,64,128]{3,2,1,0:T(8,128)S(1)}, ...), condition=%wide.region_6.0_spmd, body=%wide.region_5.0_spmd.sunk | while | flops 4200450 | bytes 3777949 | solution.py:40
  145.9 2.5 fusion.99
  158.8 2.5 fusion.99
  165.3 2.5 fusion.99
  171.7 2.5 fusion.99
  178.2 2.5 fusion.99
  184.6 2.5 fusion.99
  246.5 20.7 %all-gather.2 = f32[16,1,128]{2,1,0:T(1,128)S(1)} all-gather(f32[1,1,128]{2,1,0:T(1,128)S(1)} %bitcast.299), channel_id=2, replica_groups=mesh['row'=8,'col'=16] {'col'}, dimensions={0}, use_global_device_ids=true | all-gather | bytes 8704 | tf_op jit(solution)/shard_map/all_gather | solution.py:145
  268.0 13.1 %all_gather.27 = bf16[1024,256]{1,0:T(8,128)(2,1)S(1)} all-gather(bf16[128,256]{1,0:T(8,128)(2,1)S(1)} %multiply_convert_fusion.1), channel_id=1, replica_groups=mesh['row'=8,'col'=16] {'row'}, dimensions={0}, use_global_device_ids=true | all-gather | bytes 589824 | tf_op jit(solution)/shard_map/all_gather | solution.py:153
  283.2 70.6 %reduce-scatter.17.cloned.1.call-done = bf16[64,256]{1,0:T(8,128)(2,1)} async-done(((bf16[1024,256]{1,0:T(8,128)(2,1)}), bf16[64,256]{1,0:T(8,128)(2,1)}) %reduce-scatter.17.cloned.1.call-update) | async-done | bytes 32784 | tf_op jit(solution)/shard_map/reduce_scatter | solution.py:157
  354.5 23.3 %all_gather.28 = bf16[1024,256]{1,0:T(8,128)(2,1)S(1)} all-gather(bf16[64,256]{1,0:T(8,128)(2,1)S(1)} %add_convert_fusion.1), channel_id=1, replica_groups=mesh['row'=8,'col'=16] {'col'}, dimensions={0}, use_global_device_ids=true | all-gather | bytes 557056 | tf_op jit(solution)/shard_map/all_gather | solution.py:99
  384.2 13.3 %reshape.299 = bf16[128,32768]{1,0:T(8,128)(2,1)} reshape(bf16[8,16,4,64,128]{4,3,2,1,0:T(8,128)(2,1)} %bitcast.251) | data formatting | bytes 16777216 | tf_op jit(solution)/shard_map/reshape | solution.py:163
  397.5 4.7 fusion.2
  404.3 12.6 %all-reduce.1 = f32[1024]{0:T(1024)S(1)} all-reduce(f32[1024]{0:T(1024)S(1)} %fusion.7), channel_id=10, replica_groups=mesh['row'=8,'col'=16] {'row'}, use_global_device_ids=true, to_apply=%region_12.13.clone | all-reduce | flops 1024 | bytes 8192
  418.2 24.2 %reduce-scatter.21.cloned.1.call-done = f32[128,256]{1,0:T(8,128)} async-done(((f32[1024,256]{1,0:T(8,128)}), f32[128,256]{1,0:T(8,128)}) %reduce-scatter.21.cloned.1.call-update) | async-done | bytes 131088 | tf_op jit(solution)/shard_map/reduce_scatter | solution.py:113
  443.6 34.4 %reduce-scatter.19.cloned.1.call-done = f32[128,512]{1,0:T(8,128)} async-done(((f32[1024,512]{1,0:T(8,128)}), f32[128,512]{1,0:T(8,128)}) %reduce-scatter.19.cloned.1.call-update) | async-done | bytes 262160 | tf_op jit(solution)/shard_map/reduce_scatter | solution.py:111
  479.5 5.4 broadcast.167.clone
  484.9 70.9 %while.29 = (s32[]{:T(128)}, f32[8,4,64,128]{3,2,1,0:T(8,128)S(1)}, f32[16,8,4,64]{3,2,1,0:T(4,128)S(1)}, bf16[16,8,4,64,128]{4,3,2,0,1:T(8,128)(2,1)}, f32[16,8...) while((s32[]{:T(128)}, f32[8,4,64,128]{3,2,1,0:T(8,128)S(1)}, ...), condition=%wide.region_16.17_spmd, body=%wide.region_15.16_spmd.sunk | while | flops 4200450 | bytes 3778445 | solution.py:40
  555.9 13.3 %reshape.300 = bf16[128,32768]{1,0:T(8,128)(2,1)} reshape(bf16[8,16,4,64,128]{4,3,2,1,0:T(8,128)(2,1)} %bitcast.249) | data formatting | bytes 16777216 | tf_op jit(solution)/shard_map/reshape | solution.py:163
  569.1 4.8 fusion.3
  576.8 7.0 all-to-all-start
  584.3 66.2 %all-gather.3 = f32[16,1,128]{2,1,0:T(1,128)S(1)} all-gather(f32[1,1,128]{2,1,0:T(1,128)S(1)} %bitcast.300), channel_id=3, replica_groups=mesh['row'=8,'col'=16] {'col'}, dimensions={0}, use_global_device_ids=true | all-gather | bytes 8704 | tf_op jit(solution)/shard_map/all_gather | solution.py:145
  650.7 19.9 %all_gather.31 = bf16[1024,256]{1,0:T(8,128)(2,1)S(1)} all-gather(bf16[128,256]{1,0:T(8,128)(2,1)S(1)} %multiply_convert_fusion), channel_id=1, replica_groups=mesh['row'=8,'col'=16] {'row'}, dimensions={0}, use_global_device_ids=true | all-gather | bytes 589824 | tf_op jit(solution)/shard_map/all_gather | solution.py:153
  671.7 13.8 %pad_maximum_fusion = bf16[2,8,16,4,64,128]{5,4,3,2,1,0:T(8,128)(2,1)} fusion(bf16[1,8,16,4,64,128]{5,4,3,2,1,0:T(8,128)(2,1)} %bitcast.250, bf16[1,8,16,4,64,128]{5,4,3,2,1,0:T(8,128)(2,1)} %bitcast.252), kind=kLoop, calls=%fused_computation.22 | loop fusion | flops 8388608 | bytes 33554432 | tf_op jit(solution)/shard_map/stack | solution.py:174
  685.6 58.6 %reduce-scatter.23.cloned.1.call-done = bf16[64,256]{1,0:T(8,128)(2,1)} async-done(((bf16[1024,256]{1,0:T(8,128)(2,1)}), bf16[64,256]{1,0:T(8,128)(2,1)}) %reduce-scatter.23.cloned.1.call-update) | async-done | bytes 32784 | tf_op jit(solution)/shard_map/reduce_scatter | solution.py:157
  745.5 6.0 copy.143
  (441 shorter events, 201.1 us)
Async XLA Ops:
  7.2 48.3 %copy-start.22 = (f32[2,4]{1,0:T(2,128)S(1)}, f32[2,4]{1,0:T(2,128)}, u32[]{:S(2)}) copy-start(f32[2,4]{1,0:T(2,128)} %param.31) | copy-start | bytes 100
  7.2 48.9 %copy-start.21 = (f32[2,256]{1,0:T(2,128)S(1)}, f32[2,256]{1,0:T(2,128)}, u32[]{:S(2)}) copy-start(f32[2,256]{1,0:T(2,128)} %param.32) | copy-start | bytes 6148
  7.2 49.5 %copy-start.25 = (f32[2,4]{1,0:T(2,128)S(1)}, f32[2,4]{1,0:T(2,128)}, u32[]{:S(2)}) copy-start(f32[2,4]{1,0:T(2,128)} %param.30) | copy-start | bytes 100
  7.2 49.5 %copy-start.24 = (f32[2,4]{1,0:T(2,128)S(1)}, f32[2,4]{1,0:T(2,128)}, u32[]{:S(2)}) copy-start(f32[2,4]{1,0:T(2,128)} %param.29) | copy-start | bytes 100
  7.2 50.0 %copy-start.8 = (f32[2,4,256]{2,1,0:T(4,128)S(1)}, f32[2,4,256]{2,1,0:T(4,128)}, u32[]{:S(2)}) copy-start(f32[2,4,256]{2,1,0:T(4,128)} %param.27) | copy-start | bytes 24580
  7.2 50.6 %copy-start.9 = (f32[2,4,256]{2,1,0:T(4,128)S(1)}, f32[2,4,256]{2,1,0:T(4,128)}, u32[]{:S(2)}) copy-start(f32[2,4,256]{2,1,0:T(4,128)} %param.28) | copy-start | bytes 24580
  7.2 51.2 %copy-start.5 = (bf16[2,8,3,256]{3,1,2,0:T(8,128)(2,1)S(1)}, bf16[2,8,3,256]{3,1,2,0:T(8,128)(2,1)}, u32[]{:S(2)}) copy-start(bf16[2,8,3,256]{3,1,2,0:T(8,128)(2,1)} %param.34) | copy-start | bytes 73732
  7.3 51.2 %copy-start.6 = (bf16[2,8,3,256]{3,1,2,0:T(8,128)(2,1)S(1)}, bf16[2,8,3,256]{3,1,2,0:T(8,128)(2,1)}, u32[]{:S(2)}) copy-start(bf16[2,8,3,256]{3,1,2,0:T(8,128)(2,1)} %param.35) | copy-start | bytes 73732
  7.3 59.2 %reduce-scatter.25.cloned.1.call-start = ((), (), s32[]{:S(2)}) async-start(), calls=%async_computation.15 | async-start | bytes 589824
  35.9 64.4 %reduce-scatter.15.cloned.1.call-start = ((), (), s32[]{:S(2)}) async-start(), calls=%async_computation.10 | async-start | bytes 1179648 | tf_op jit(solution)/shard_map/reduce_scatter | solution.py:113
  38.1 97.8 %reduce-scatter.13.cloned.1.call-start = ((), (), s32[]{:S(2)}) async-start(), calls=%async_computation.9 | async-start | bytes 2359296 | tf_op jit(solution)/shard_map/reduce_scatter | solution.py:111
  41.4 312.4 %reduce-scatter.17.cloned.1.call-start = ((), (), s32[]{:S(2)}) async-start(), calls=%async_computation.11 | async-start | bytes 557056 | tf_op jit(solution)/shard_map/reduce_scatter | solution.py:157
  142.7 211.0 %copy-start.3 = (bf16[64,256]{1,0:T(8,128)(2,1)S(1)}, bf16[64,256]{1,0:T(8,128)(2,1)}, u32[]{:S(2)}) copy-start(bf16[64,256]{1,0:T(8,128)(2,1)} %param.22) | copy-start | bytes 98308
  142.7 237.0 %copy-start.1 = (bf16[2,256,256]{2,1,0:T(8,128)(2,1)S(1)}, bf16[2,256,256]{2,1,0:T(8,128)(2,1)}, u32[]{:S(2)}) copy-start(bf16[2,256,256]{2,1,0:T(8,128)(2,1)} %param.25) | copy-start | bytes 786436
  246.1 135.7 %copy-start.7 = (f32[1,256]{1,0:T(1,128)S(1)}, f32[1,256]{1,0:T(1,128)}, u32[]{:S(2)}) copy-start(f32[1,256]{1,0:T(1,128)} %get-tuple-element.219) | copy-start | bytes 3076
  246.1 137.5 %copy-start.27 = (s32[8]{0:T(128)S(1)}, s32[8]{0:T(128)}, u32[]{:S(2)}) copy-start(s32[8]{0:T(128)} %param.38) | copy-start | bytes 100
  246.1 137.7 %copy-start.23 = (s32[4,2]{0,1:T(2,128)S(1)}, s32[4,2]{0,1:T(2,128)}, u32[]{:S(2)}) copy-start(s32[4,2]{0,1:T(2,128)} %param.39) | copy-start | bytes 100
  246.1 137.8 %copy-start.26 = (s32[8]{0:T(128)S(1)}, s32[8]{0:T(128)}, u32[]{:S(2)}) copy-start(s32[8]{0:T(128)} %param.37) | copy-start | bytes 100
  283.1 133.8 %reduce-scatter.27.cloned.1.call-start = ((), (), s32[]{:S(2)}) async-start(), calls=%async_computation.16 | async-start | bytes 589824
  379.7 62.8 %reduce-scatter.21.cloned.1.call-start = ((), (), s32[]{:S(2)}) async-start(), calls=%async_computation.13 | async-start | bytes 1179648 | tf_op jit(solution)/shard_map/reduce_scatter | solution.py:113
  381.7 96.4 %reduce-scatter.19.cloned.1.call-start = ((), (), s32[]{:S(2)}) async-start(), calls=%async_computation.12 | async-start | bytes 2359296 | tf_op jit(solution)/shard_map/reduce_scatter | solution.py:111
  397.5 46.0 %copy-start.15 = (f32[1,1,256]{2,1,0:T(1,128)S(1)}, f32[1,1,256]{2,1,0:T(1,128)}, u32[]{:S(2)}) copy-start(f32[1,1,256]{2,1,0:T(1,128)} %get-tuple-element.202) | copy-start | bytes 3076
  397.5 46.0 %copy-start.16 = (f32[1,1,256]{2,1,0:T(1,128)S(1)}, f32[1,1,256]{2,1,0:T(1,128)}, u32[]{:S(2)}) copy-start(f32[1,1,256]{2,1,0:T(1,128)} %get-tuple-element.207) | copy-start | bytes 3076
  397.5 46.0 %copy-start.17 = (f32[1,1,256]{2,1,0:T(1,128)S(1)}, f32[1,1,256]{2,1,0:T(1,128)}, u32[]{:S(2)}) copy-start(f32[1,1,256]{2,1,0:T(1,128)} %get-tuple-element.208) | copy-start | bytes 3076
  397.5 81.7 %copy-start.10 = (f32[1,1,256]{2,1,0:T(1,128)S(1)}, f32[1,1,256]{2,1,0:T(1,128)}, u32[]{:S(2)}) copy-start(f32[1,1,256]{2,1,0:T(1,128)} %get-tuple-element.209) | copy-start | bytes 3076
  397.5 81.7 %copy-start.11 = (f32[1,1,256]{2,1,0:T(1,128)S(1)}, f32[1,1,256]{2,1,0:T(1,128)}, u32[]{:S(2)}) copy-start(f32[1,1,256]{2,1,0:T(1,128)} %get-tuple-element.210) | copy-start | bytes 3076
  397.5 81.7 %copy-start.12 = (f32[1,1,256]{2,1,0:T(1,128)S(1)}, f32[1,1,256]{2,1,0:T(1,128)}, u32[]{:S(2)}) copy-start(f32[1,1,256]{2,1,0:T(1,128)} %get-tuple-element.215) | copy-start | bytes 3076
  397.5 81.7 %copy-start.13 = (f32[1,1,256]{2,1,0:T(1,128)S(1)}, f32[1,1,256]{2,1,0:T(1,128)}, u32[]{:S(2)}) copy-start(f32[1,1,256]{2,1,0:T(1,128)} %get-tuple-element.216) | copy-start | bytes 3076
  574.4 76.1 %copy-start.18 = (f32[1,256]{1,0:T(1,128)S(1)}, f32[1,256]{1,0:T(1,128)}, u32[]{:S(2)}) copy-start(f32[1,256]{1,0:T(1,128)} %get-tuple-element.217) | copy-start | bytes 3076
  574.5 96.2 %copy-start.2 = (bf16[2,256,256]{2,1,0:T(8,128)(2,1)S(1)}, bf16[2,256,256]{2,1,0:T(8,128)(2,1)}, u32[]{:S(2)}) copy-start(bf16[2,256,256]{2,1,0:T(8,128)(2,1)} %param.33) | copy-start | bytes 786436
  576.8 168.7 %all-to-all-start = ((bf16[16,2,2,4,64,128]{5,4,3,1,2,0:T(8,128)(2,1)}), bf16[16,2,2,4,64,128]{5,4,3,1,2,0:T(8,128)(2,1)}, u32[]{:S(2)}, u32[]{:S(2)}) async-start(bf16[16,2,2,4,64,128]{5,4,3,1,2,0:T(8,128)(2,1)} %pad_maximum_fusion.1), calls=%async_computation.6 | async-start | bytes 8388608 | tf_op jit(solution)/shard_map/all_to_all | solution.py:170
  583.9 160.2 %reduce-scatter.23.cloned.1.call-start = ((), (), s32[]{:S(2)}) async-start(), calls=%async_computation.14 | async-start | bytes 557056 | tf_op jit(solution)/shard_map/reduce_scatter | solution.py:157
  (6 other events, 172.6 us)
Sparse Core Ops, SparseCore 0:
  36.0 30.4 reduce-scatter.24
  69.5 30.7 reduce-scatter.14
  103.4 32.4 reduce-scatter.12
  283.3 70.4 reduce-scatter.16
  379.8 29.4 reduce-scatter.26
  411.6 30.7 reduce-scatter.20
  445.5 32.5 reduce-scatter.18
  671.9 72.2 reduce-scatter.22
